TPU v7x, 32 devices: a whole 2x2x4 slice. The times are simulated.
32 devices in a mesh: seq: 16 (over z, y, core), blk: 2 (over x).
Axes of the slice: x: 2, y: 2, z: 4, core: 2. Of those that a mesh axis runs over, the one named last changes fastest.
Arguments:
- tokens: bfloat16 [32, 1024, 512], P('seq', 'blk'), may hold values from -6 to 6
- memory: bfloat16 [32, 512, 512], P('seq', 'blk'), may hold values from -6 to 6
- segment_ends: int32 [32, 1024], P('seq', 'blk'), may hold values from 1 to 8192, as said below
- memory_ends: int32 [32, 512], P('seq', 'blk'), may hold values from -4088 to 0, as said below
- segment_counts: int32 [32], P('seq'), may hold values from 512 to 1024, as said below
- memory_lengths: int32 [32], P('seq'), may hold values from 128 to 512, as said below
- first_gain: float32 [512], replicated, may hold values from 0.5 to 1.5
- first_shift: float32 [512], replicated, may hold values from -1.2 to 1.2
- query_weight: bfloat16 [512, 512], replicated, may hold values from -0.25 to 0.25
- key_weight: bfloat16 [512, 512], replicated, may hold values from -0.25 to 0.25
- value_weight: bfloat16 [512, 512], replicated, may hold values from -0.25 to 0.25
- out_weight: bfloat16 [512, 512], replicated, may hold values from -2 to 2
- head_slopes: float32 [8], replicated, may hold values from 1e-05 to 0.03
- second_gain: float32 [512], replicated, may hold values from 0.5 to 1.5
- second_shift: float32 [512], replicated, may hold values from -1.2 to 1.2
- hidden_weight: bfloat16 [512, 2048], replicated, may hold values from -0.25 to 0.25
- output_weight: bfloat16 [2048, 512], replicated, may hold values from -0.125 to 0.125
- output_grad: bfloat16 [32, 1024, 512], P('seq', 'blk'), may hold values from -6 to 6
Outputs:
- layer_out: bfloat16 [32, 1024, 512], P('seq', 'blk')
- input_grad: bfloat16 [32, 1024, 512], P('seq', 'blk')
- grad_first_gain: float32 [512], replicated
- grad_first_shift: float32 [512], replicated
- grad_query_weight: float32 [512, 512], replicated
- grad_key_weight: float32 [512, 512], replicated
- grad_value_weight: float32 [512, 512], replicated
- grad_out_weight: float32 [512, 512], replicated
- grad_head_slopes: float32 [8], replicated
- grad_second_gain: float32 [512], replicated
- grad_second_shift: float32 [512], replicated
- grad_hidden_weight: float32 [512, 2048], replicated
- grad_output_weight: float32 [2048, 512], replicated
Inputs may be any that keep to these rules, and one draw needn't show every extreme that they name: `segment_ends`: each row rises strictly by 1 to 8 bytes from slot to slot; the first slot ends 1 to 8 bytes after the row's last memory end. In some sequence every step is 8 bytes; in another the first slot ends 1 byte after its memory. `memory_ends`: each row rises strictly by 1 to 8 bytes from entry to entry and its last entry is 0; in some sequence every step is 8 bytes. `segment_counts`: slots 0 to count - 1 of a sequence hold segments, the others are empty; some sequence uses all 1024 slots and some exactly half of them. `memory_lengths`: the last length memory rows of a sequence are valid; some sequence has all 512 and some a quarter.
All inputs are finite; a program needn't handle non-finite values.
Results may differ from a plain program's by a relative error of at most 0.022.
Values may be sent and summed in bfloat16 or wider, within the bound.
A program may use at most 256 MiB of HBM per device.

v0:
```python
import math
import jax
import jax.numpy as jnp
from jax import lax
from jax.sharding import PartitionSpec as P

epsilon = 1e-05
far_order = 1073741824


def layer_norm(values, gain, shift):
    centred = values - jnp.mean(values, axis=-1, keepdims=True)
    spread = jnp.mean(centred * centred, axis=-1, keepdims=True)
    return centred * lax.rsqrt(spread + epsilon) * gain + shift


def block_scores(
    q_heads, key_block, q_ends, key_order, key_ends, q_index, head_slopes, score_scale
):
    scores = (
        jnp.einsum("qhd,khd->hqk", q_heads, key_block, preferred_element_type=jnp.float32)
        * score_scale
    )
    distance = (q_ends[:, None] - key_ends[None, :]).astype(jnp.float32)
    scores = scores - head_slopes[:, None, None] * distance[None]
    allowed = key_order[None, :] <= q_index[:, None]
    return (jnp.where(allowed[None], scores, -1e30), distance)


def per_device(
    tokens,
    memory,
    segment_ends,
    memory_ends,
    segment_counts,
    memory_lengths,
    first_gain,
    first_shift,
    query_weight,
    key_weight,
    value_weight,
    out_weight,
    head_slopes,
    second_gain,
    second_shift,
    hidden_weight,
    output_weight,
    output_grad,
):
    seq_count, slot_count, model_width = tokens.shape
    mem_count = memory.shape[1]
    head_count = head_slopes.shape[0]
    head_dim = model_width // head_count
    score_scale = 1.0 / math.sqrt(head_dim)
    key_rows = mem_count + slot_count
    blocks = lax.axis_size("blk")
    my_block = lax.axis_index("blk")
    x_float = tokens.astype(jnp.float32)
    mem_float = memory.astype(jnp.float32)
    normed = layer_norm(x_float, first_gain, first_shift).astype(jnp.bfloat16)
    mem_normed = layer_norm(mem_float, first_gain, first_shift).astype(jnp.bfloat16)
    key_input = jnp.concatenate([mem_normed, normed], axis=1)
    query = jnp.einsum(
        "std,de->ste", normed, query_weight, preferred_element_type=jnp.float32
    ).astype(jnp.bfloat16)
    pair_weight = jnp.concatenate([key_weight, value_weight], axis=1)
    key_value = jnp.einsum(
        "srd,de->rse", key_input, pair_weight, preferred_element_type=jnp.float32
    ).astype(jnp.bfloat16)
    mem_index = my_block * mem_count + jnp.arange(mem_count, dtype=jnp.int32)
    slot_index = my_block * slot_count + jnp.arange(slot_count, dtype=jnp.int32)
    mem_order = jnp.where(
        mem_index[None, :] >= mem_count * blocks - memory_lengths[:, None], -1, far_order
    )
    slot_order = jnp.where(
        slot_index[None, :] < segment_counts[:, None], slot_index[None, :], far_order
    )
    key_meta = jnp.stack(
        [
            jnp.concatenate([mem_order, slot_order], axis=1),
            jnp.concatenate([memory_ends, segment_ends], axis=1),
        ]
    )
    all_pairs, all_meta = (
        lax.all_gather(key_value, "blk", axis=0, tiled=True),
        lax.all_gather(key_meta, "blk", axis=2, tiled=True),
    )
    query_heads = query.reshape(seq_count, slot_count, head_count, head_dim)

    def pick(seq_index):
        pair_rows = lax.dynamic_index_in_dim(all_pairs, seq_index, 1, keepdims=False)
        meta_rows = lax.dynamic_index_in_dim(all_meta, seq_index, 1, keepdims=False)
        key_heads = pair_rows[:, :model_width].reshape(-1, key_rows, head_count, head_dim)
        value_heads = pair_rows[:, model_width:].reshape(-1, key_rows, head_count, head_dim)
        return (
            key_heads,
            value_heads,
            meta_rows[0].reshape(-1, key_rows),
            meta_rows[1].reshape(-1, key_rows),
        )

    def attend(seq_index):
        key_heads, value_heads, key_order, key_ends = pick(seq_index)
        q_heads = lax.dynamic_index_in_dim(query_heads, seq_index, 0, keepdims=False)
        q_ends = lax.dynamic_index_in_dim(segment_ends, seq_index, 0, keepdims=False)

        def stats_step(running, pieces):
            scores = block_scores(
                q_heads,
                pieces[0],
                q_ends,
                pieces[1],
                pieces[2],
                slot_index,
                head_slopes,
                score_scale,
            )[0]
            running_max = jnp.maximum(running[0], jnp.max(scores, axis=-1))
            running_sum = running[1] * jnp.exp(running[0] - running_max) + jnp.sum(
                jnp.exp(scores - running_max[..., None]), axis=-1
            )
            return ((running_max, running_sum), None)

        start_max = jnp.full((head_count, slot_count), -jnp.inf, jnp.float32)
        (top_max, top_sum), _ = lax.scan(
            stats_step, (start_max, jnp.zeros_like(start_max)), (key_heads, key_order, key_ends)
        )
        log_total = top_max + jnp.log(top_sum)

        def out_step(summed, pieces):
            scores = block_scores(
                q_heads,
                pieces[0],
                q_ends,
                pieces[1],
                pieces[2],
                slot_index,
                head_slopes,
                score_scale,
            )[0]
            attn_probs = jnp.exp(scores - log_total[..., None]).astype(jnp.bfloat16)
            return (
                summed
                + jnp.einsum(
                    "hqk,khd->qhd", attn_probs, pieces[3], preferred_element_type=jnp.float32
                ),
                None,
            )

        start_out = jnp.zeros((slot_count, head_count, head_dim), jnp.float32)
        mixed_heads, _ = lax.scan(
            out_step, start_out, (key_heads, key_order, key_ends, value_heads)
        )
        return (mixed_heads, log_total)

    mixed_all, log_totals = lax.map(attend, jnp.arange(seq_count))
    mixed_low = mixed_all.reshape(seq_count, slot_count, model_width).astype(jnp.bfloat16)
    residual = x_float + jnp.einsum(
        "std,de->ste", mixed_low, out_weight, preferred_element_type=jnp.float32
    )
    second_low = layer_norm(residual, second_gain, second_shift).astype(jnp.bfloat16)
    hidden_pre = jnp.einsum(
        "std,df->stf", second_low, hidden_weight, preferred_element_type=jnp.float32
    )
    act_low = jax.nn.gelu(hidden_pre, approximate=False).astype(jnp.bfloat16)
    layer_out = (
        residual
        + jnp.einsum("stf,fd->std", act_low, output_weight, preferred_element_type=jnp.float32)
    ).astype(jnp.bfloat16)
    grad_output_w = jnp.einsum(
        "stf,std->fd", act_low, output_grad, preferred_element_type=jnp.float32
    )
    d_act = jnp.einsum(
        "std,fd->stf", output_grad, output_weight, preferred_element_type=jnp.float32
    )
    _, gelu_pull = jax.vjp(lambda inner: jax.nn.gelu(inner, approximate=False), hidden_pre)
    d_pre_low = gelu_pull(d_act)[0].astype(jnp.bfloat16)
    grad_hidden_w = jnp.einsum(
        "std,stf->df", second_low, d_pre_low, preferred_element_type=jnp.float32
    )
    d_second = jnp.einsum(
        "stf,df->std", d_pre_low, hidden_weight, preferred_element_type=jnp.float32
    )
    _, second_pull = jax.vjp(layer_norm, residual, second_gain, second_shift)
    d_resid_norm, grad_second_g, grad_second_b = second_pull(d_second)
    d_residual = d_resid_norm + output_grad.astype(jnp.float32)
    d_branch = d_residual.astype(jnp.bfloat16)
    grad_out_w = jnp.einsum("std,ste->de", mixed_low, d_branch, preferred_element_type=jnp.float32)
    d_mixed = jnp.einsum(
        "ste,de->std", d_branch, out_weight, preferred_element_type=jnp.float32
    ).astype(jnp.bfloat16)
    d_mixed_heads = d_mixed.reshape(seq_count, slot_count, head_count, head_dim)

    def query_side(seq_index):
        key_heads, value_heads, key_order, key_ends = pick(seq_index)
        q_heads = lax.dynamic_index_in_dim(query_heads, seq_index, 0, keepdims=False)
        q_ends = lax.dynamic_index_in_dim(segment_ends, seq_index, 0, keepdims=False)
        d_heads = lax.dynamic_index_in_dim(d_mixed_heads, seq_index, 0, keepdims=False)
        log_total = lax.dynamic_index_in_dim(log_totals, seq_index, 0, keepdims=False)

        def probs_of(key_block, order_block, ends_block, value_block):
            scores, distance = block_scores(
                q_heads,
                key_block,
                q_ends,
                order_block,
                ends_block,
                slot_index,
                head_slopes,
                score_scale,
            )
            attn_probs = jnp.exp(scores - log_total[..., None])
            d_probs = jnp.einsum(
                "qhd,khd->hqk", d_heads, value_block, preferred_element_type=jnp.float32
            )
            return (attn_probs, d_probs, distance)

        def delta_step(summed, pieces):
            attn_probs, d_probs, _ = probs_of(pieces[0], pieces[1], pieces[2], pieces[3])
            return (summed + jnp.sum(attn_probs * d_probs, axis=-1), None)

        delta_rows, _ = lax.scan(
            delta_step,
            jnp.zeros((head_count, slot_count), jnp.float32),
            (key_heads, key_order, key_ends, value_heads),
        )

        def grad_step(running, pieces):
            attn_probs, d_probs, distance = probs_of(pieces[0], pieces[1], pieces[2], pieces[3])
            d_scores = (attn_probs * (d_probs - delta_rows[..., None])).astype(jnp.bfloat16)
            d_query = running[0] + jnp.einsum(
                "hqk,khd->qhd", d_scores, pieces[0], preferred_element_type=jnp.float32
            )
            d_slopes = running[1] - jnp.sum(
                d_scores.astype(jnp.float32) * distance[None], axis=(1, 2)
            )
            return ((d_query, d_slopes), None)

        start_grads = (
            jnp.zeros((slot_count, head_count, head_dim), jnp.float32),
            jnp.zeros((head_count,), jnp.float32),
        )
        (d_query, d_slopes), _ = lax.scan(
            grad_step, start_grads, (key_heads, key_order, key_ends, value_heads)
        )
        return (d_query * score_scale, delta_rows, d_slopes)

    d_query_all, delta_all, slope_parts = lax.map(query_side, jnp.arange(seq_count))
    grad_slopes = jnp.sum(slope_parts, axis=0)
    d_query_low = d_query_all.reshape(seq_count, slot_count, model_width).astype(jnp.bfloat16)

    def pair_terms(
        pair_rows, order_block, ends_block, q_heads, q_ends, q_index, d_heads, log_total, delta_rows
    ):
        key_block = pair_rows[:, :model_width].reshape(key_rows, head_count, head_dim)
        value_block = pair_rows[:, model_width:].reshape(key_rows, head_count, head_dim)
        scores, _ = block_scores(
            q_heads, key_block, q_ends, order_block, ends_block, q_index, head_slopes, score_scale
        )
        attn_probs = jnp.exp(scores - log_total[..., None])
        d_probs = jnp.einsum(
            "qhd,khd->hqk", d_heads, value_block, preferred_element_type=jnp.float32
        )
        d_scores = (attn_probs * (d_probs - delta_rows[..., None])).astype(jnp.bfloat16)
        d_value = jnp.einsum(
            "hqk,qhd->khd",
            attn_probs.astype(jnp.bfloat16),
            d_heads,
            preferred_element_type=jnp.float32,
        )
        d_key = (
            jnp.einsum("hqk,qhd->khd", d_scores, q_heads, preferred_element_type=jnp.float32)
            * score_scale
        )
        return jnp.concatenate(
            [d_key.reshape(key_rows, model_width), d_value.reshape(key_rows, model_width)], axis=1
        )

    def one_block(block_index):
        offset = block_index * key_rows
        pair_block = lax.dynamic_slice_in_dim(all_pairs, offset, key_rows, 0)
        meta_block = lax.dynamic_slice_in_dim(all_meta, offset, key_rows, 2)
        return jax.vmap(pair_terms, in_axes=(1, 0, 0, 0, 0, None, 0, 0, 0), out_axes=1)(
            pair_block,
            meta_block[0],
            meta_block[1],
            query_heads,
            segment_ends,
            slot_index,
            d_mixed_heads,
            log_totals,
            delta_all,
        )

    pieces = lax.map(one_block, jnp.arange(lax.axis_size("blk") * key_rows // key_rows))
    pair_grads = lax.psum_scatter(
        pieces.reshape(lax.axis_size("blk") * key_rows, seq_count, 2 * model_width).astype(
            jnp.bfloat16
        ),
        "blk",
        scatter_dimension=0,
        tiled=True,
    )
    grad_pair_w = jnp.einsum(
        "srd,rse->de", key_input, pair_grads, preferred_element_type=jnp.float32
    )
    grad_key_w = grad_pair_w[:, :model_width]
    grad_value_w = grad_pair_w[:, model_width:]
    d_key_input = jnp.einsum(
        "rse,de->srd", pair_grads, pair_weight, preferred_element_type=jnp.float32
    )
    grad_query_w = jnp.einsum(
        "std,ste->de", normed, d_query_low, preferred_element_type=jnp.float32
    )
    d_normed = (
        jnp.einsum("ste,de->std", d_query_low, query_weight, preferred_element_type=jnp.float32)
        + d_key_input[:, mem_count:]
    )
    _, first_pull = jax.vjp(layer_norm, x_float, first_gain, first_shift)
    d_tokens, gain_slots, shift_slots = first_pull(d_normed)
    _, mem_pull = jax.vjp(
        lambda gain, shift: layer_norm(mem_float, gain, shift), first_gain, first_shift
    )
    gain_mem, shift_mem = mem_pull(d_key_input[:, :mem_count])
    input_grad = (d_tokens + d_residual).astype(jnp.bfloat16)
    grad_first_g = gain_slots + gain_mem
    grad_first_b = shift_slots + shift_mem
    summed = lax.psum(
        (
            grad_first_g,
            grad_first_b,
            grad_query_w,
            grad_key_w,
            grad_value_w,
            grad_out_w,
            grad_slopes,
            grad_second_g,
            grad_second_b,
            grad_hidden_w,
            grad_output_w,
        ),
        ("seq", "blk"),
    )
    return (
        layer_out,
        input_grad,
        summed[0],
        summed[1],
        summed[2],
        summed[3],
        summed[4],
        summed[5],
        summed[6],
        summed[7],
        summed[8],
        summed[9],
        summed[10],
    )


def solution(mesh):
    placed = (
        P("seq", "blk", None),
        P("seq", "blk", None),
        P("seq", "blk"),
        P("seq", "blk"),
        P("seq"),
        P("seq"),
        P(),
        P(),
        P(),
        P(),
        P(),
        P(),
        P(),
        P(),
        P(),
        P(),
        P(),
        P("seq", "blk", None),
    )
    return jax.shard_map(
        per_device,
        mesh=mesh,
        in_specs=placed,
        out_specs=(
            P("seq", "blk", None),
            P("seq", "blk", None),
            P(),
            P(),
            P(),
            P(),
            P(),
            P(),
            P(),
            P(),
            P(),
            P(),
            P(),
        ),
        check_vma=False,
    )
```

profile of v0, /device:TPU:0, one launch (start us, length us, event | category | flops | bytes accessed | tf_op | source)
XLA Modules:
  0.0 937.2 jit_solution(17816046465124142338)
XLA Ops:
  26.0 5.4 all_gather.7
  34.2 73.6 %all-gather.2.cloned.1.call-done = bf16[1536,2,1024]{0,2,1:T(8,128)(2,1)} async-done(((bf16[768,2,1024]{0,2,1:T(8,128)(2,1)}), bf16[1536,2,1024]{0,2,1:T(8,128)(2,1)}) %all-gather.2.cloned.1.call-update) | async-done | bytes 6291472 | tf_op jit(solution)/shard_map/all_gather | solution.py:85
  110.0 168.7 %while.93 = (s32[]{:T(128)}, bf16[2,512,8,64]{1,3,2,0:T(8,128)(2,1)}, f32[2,8,512]{2,1,0:T(8,128)}, s32[2]{0:T(128)}, bf16[1536,2,1024]{0,2,1:T(8,128)(2,1)}, /*...) while((s32[]{:T(128)}, ...), condition=%wide.region_11.12_spmd.clone, body=%wide.region_4.11_spmd.clone.sunk | while | flops 1264345600 | bytes 82579288 | solution.py:156
  123.6 4.6 reshape.453
  138.4 21.8 %while.98 = (s32[]{:T(128)}, f32[8,512]{1,0:T(8,128)S(1)}, f32[8,512]{1,0:T(8,128)S(1)}, s32[2,768]{1,0:T(2,128)S(1)}, s32[512]{0:T(512)S(1)}, /*index=5*/bf16[2...) while((s32[]{:T(128)}, f32[8,512]{1,0:T(8,128)S(1)}, ...), condition=%wide.region_8.8_spmd.clone, body=%wide.region_5.7_spmd.clone.sunk | while | flops 438456320 | bytes 32610988 | solution.py:125
  139.6 5.3 fusion.232
  150.5 5.3 fusion.232
  160.9 31.5 %while.99 = (s32[]{:T(128)}, f32[512,8,64]{0,2,1:T(8,128)}, bf16[2,768,8,64]{1,3,2,0:T(8,128)(2,1)}, s32[2,768]{1,0:T(2,128)S(1)}, s32[512]{0:T(512)S(1)}, /*ind...) while((s32[]{:T(128)}, f32[512,8,64]{0,2,1:T(8,128)}, ...), condition=%wide.region_10.10_spmd.clone, body=%wide.region_9.9_spmd.clone.sunk | while | flops 825884672 | bytes 19438292 | solution.py:151
  167.6 8.0 fusion.238
  183.4 8.1 fusion.238
  207.6 4.6 reshape.453
  222.5 21.8 %while.98 = (s32[]{:T(128)}, f32[8,512]{1,0:T(8,128)S(1)}, f32[8,512]{1,0:T(8,128)S(1)}, s32[2,768]{1,0:T(2,128)S(1)}, s32[512]{0:T(512)S(1)}, /*index=5*/bf16[2...) while((s32[]{:T(128)}, f32[8,512]{1,0:T(8,128)S(1)}, ...), condition=%wide.region_8.8_spmd.clone, body=%wide.region_5.7_spmd.clone.sunk | while | flops 438456320 | bytes 32610988 | solution.py:125
  223.7 5.3 fusion.232
  234.5 5.3 fusion.232
  244.9 31.5 %while.99 = (s32[]{:T(128)}, f32[512,8,64]{0,2,1:T(8,128)}, bf16[2,768,8,64]{1,3,2,0:T(8,128)(2,1)}, s32[2,768]{1,0:T(2,128)S(1)}, s32[512]{0:T(512)S(1)}, /*ind...) while((s32[]{:T(128)}, f32[512,8,64]{0,2,1:T(8,128)}, ...), condition=%wide.region_10.10_spmd.clone, body=%wide.region_9.9_spmd.clone.sunk | while | flops 825884672 | bytes 19438292 | solution.py:151
  251.6 8.1 fusion.238
  267.4 8.1 fusion.238
  286.0 20.1 %multiply_convert_fusion = (bf16[2,512,2048]{2,1,0:T(8,128)(2,1)}, f32[2,512,2048]{2,1,0:T(8,128)}) fusion(f32[2,512,2048]{2,1,0:T(8,128)S(1)} %get-tuple-element.1058, u8[512,2048]{1,0:T(8,128)(4,1)S(1)} %get-tuple-element.841, u8[512,2048]{1,0:T(8,128)(4,1)S(1)} %get-tuple-element.840), kind=kLoop, calls=%fused_computation.134 | loop fusion | flops 146800640 | bytes 23068672 | tf_op jit(solution)/shard_map/convert_element_type | solution.py:165
  306.1 6.8 add_convert_fusion
  322.6 155.2 %while.96 = (s32[]{:T(128)}, bf16[2,512,8,64]{1,3,2,0:T(8,128)(2,1)}, f32[2,8,512]{2,1,0:T(8,128)}, f32[2,8]{1,0:T(2,128)}, s32[2]{0:T(128)}, /*index=5*/bf16[15...) while((s32[]{:T(128)}, ...), condition=%wide.region_23.24_spmd.clone, body=%wide.region_16.23_spmd.clone.sunk | while | flops 2073039360 | bytes 125587736 | solution.py:248
  334.2 4.7 copy.151
  348.6 5.2 reshape.456
  358.2 18.1 %while.100 = (s32[]{:T(128)}, f32[8,512]{1,0:T(8,128)S(1)}, s32[2,768]{1,0:T(2,128)S(1)}, s32[512]{0:T(512)S(1)}, bf16[2,768,8,64]{1,3,2,0:T(8,128)(2,1)S(1)}, /...) while((s32[]{:T(128)}, f32[8,512]{1,0:T(8,128)S(1)}, ...), condition=%wide.region_19.19_spmd.clone, body=%wide.region_17.18_spmd.clone.sunk | while | flops 828510208 | bytes 40212728 | solution.py:222
  360.5 6.6 fusion.222
  369.6 6.6 fusion.222
  376.3 23.0 %while.101 = (s32[]{:T(128)}, f32[512,8,64]{0,2,1:T(8,128)S(1)}, f32[8]{0:T(128)S(1)}, bf16[2,768,8,64]{1,3,2,0:T(8,128)(2,1)S(1)}, s32[2,768]{1,0:T(2,128)S(1)}...) while((s32[]{:T(128)}, f32[512,8,64]{0,2,1:T(8,128)S(1)}, ...), condition=%wide.region_22.22_spmd.clone, body=%wide.region_20.21_spmd.clone.sunk | while | flops 1244266496 | bytes 49339216 | solution.py:243
  378.6 7.8 multiply_reduce_fusion.5
  390.1 7.8 multiply_reduce_fusion.5
  411.6 4.7 copy.151
  425.9 5.2 reshape.456
  435.5 18.1 %while.100 = (s32[]{:T(128)}, f32[8,512]{1,0:T(8,128)S(1)}, s32[2,768]{1,0:T(2,128)S(1)}, s32[512]{0:T(512)S(1)}, bf16[2,768,8,64]{1,3,2,0:T(8,128)(2,1)S(1)}, /...) while((s32[]{:T(128)}, f32[8,512]{1,0:T(8,128)S(1)}, ...), condition=%wide.region_19.19_spmd.clone, body=%wide.region_17.18_spmd.clone.sunk | while | flops 828510208 | bytes 40212728 | solution.py:222
  437.9 6.6 fusion.222
  446.9 6.6 fusion.222
  453.6 23.0 %while.101 = (s32[]{:T(128)}, f32[512,8,64]{0,2,1:T(8,128)S(1)}, f32[8]{0:T(128)S(1)}, bf16[2,768,8,64]{1,3,2,0:T(8,128)(2,1)S(1)}, s32[2,768]{1,0:T(2,128)S(1)}...) while((s32[]{:T(128)}, f32[512,8,64]{0,2,1:T(8,128)S(1)}, ...), condition=%wide.region_22.22_spmd.clone, body=%wide.region_20.21_spmd.clone.sunk | while | flops 1244266496 | bytes 49339216 | solution.py:243
  456.0 7.8 multiply_reduce_fusion.5
  467.5 7.8 multiply_reduce_fusion.5
  477.8 116.6 %while.97 = (s32[]{:T(128)}, bf16[2,768,2,1024]{3,1,0,2:T(8,128)(2,1)}, s32[2]{0:T(128)S(1)}, s32[2,2,1536]{2,1,0:T(2,128)}, bf16[1536,2,1024]{0,2,1:T(8,128)(2,...) while((s32[]{:T(128)}, ...), condition=%wide.region_25.26_spmd.clone, body=%wide.region_24.25_spmd.clone.sunk | while | flops 3319529984 | bytes 129511832 | solution.py:295
  485.4 11.3 %fusion.214 = f32[2,8,768,512]{3,2,1,0:T(8,128)} fusion(bf16[2,768,8,64]{1,3,2,0:T(8,128)(2,1)S(1)} %bitcast.354, bf16[2,512,8,64]{1,3,2,0:T(8,128)(2,1)} %get-tuple-element.2049), kind=kOutput, calls=%fused_computation.237.clone.1 | convolution fusion | flops 805306368 | bytes 27787264 | tf_op jit(solution)/shard_map/while/body/eval_jaxpr/vmap(qhd,khd->hqk)/dot_general | solution.py:21
  496.8 19.0 %fusion.216 = bf16[2,8,768,64]{2,3,1,0:T(8,128)(2,1)} fusion(bf16[2,512,8,64]{1,3,2,0:T(8,128)(2,1)} %get-tuple-element.2049, f32[2,8,768,512]{3,2,1,0:T(8,128)} %fusion.214, f32[2,8,512]{2,1,0:T(8,128)S(1)} %copy-done.60, f32[2,8,512]{2,1,0:T(8,128)} %get-tuple-element.2052, f32[2,512,768]{1,2,0:T(8,128)S(1)} %subtract_convert_fusion.10, ...), kind=kOutput, calls=%fused_computation.15.clone.1 | convolution fusion | flops 1662517248 | bytes 34406432 | tf_op jit(solution)/shard_map/while/body/eval_jaxpr/vmap(hqk,qhd->khd)/dot_general | solution.py:272
  515.8 13.2 %fusion.215 = bf16[2,8,768,64]{2,3,1,0:T(8,128)(2,1)S(1)} fusion(bf16[2,512,8,64]{1,3,2,0:T(8,128)(2,1)} %get-tuple-element.2053, f32[2,8,768,512]{3,2,1,0:T(8,128)} %fusion.214, f32[2,8,512]{2,1,0:T(8,128)} %get-tuple-element.2052, f32[2,512,768]{1,2,0:T(8,128)S(1)} %subtract_convert_fusion.10, f32[8]{0:T(128)} %get-tuple-element.2050, ...), kind=kOutput, calls=%fused_computation.10.clone.1 | convolution fusion | flops 843055104 | bytes 31752224 | tf_op jit(solution)/shard_map/while/body/eval_jaxpr/vmap(hqk,qhd->khd)/dot_general | solution.py:265
  543.7 11.3 %fusion.214 = f32[2,8,768,512]{3,2,1,0:T(8,128)} fusion(bf16[2,768,8,64]{1,3,2,0:T(8,128)(2,1)S(1)} %bitcast.354, bf16[2,512,8,64]{1,3,2,0:T(8,128)(2,1)} %get-tuple-element.2049), kind=kOutput, calls=%fused_computation.237.clone.1 | convolution fusion | flops 805306368 | bytes 27787264 | tf_op jit(solution)/shard_map/while/body/eval_jaxpr/vmap(qhd,khd->hqk)/dot_general | solution.py:21
  555.0 19.0 %fusion.216 = bf16[2,8,768,64]{2,3,1,0:T(8,128)(2,1)} fusion(bf16[2,512,8,64]{1,3,2,0:T(8,128)(2,1)} %get-tuple-element.2049, f32[2,8,768,512]{3,2,1,0:T(8,128)} %fusion.214, f32[2,8,512]{2,1,0:T(8,128)S(1)} %copy-done.60, f32[2,8,512]{2,1,0:T(8,128)} %get-tuple-element.2052, f32[2,512,768]{1,2,0:T(8,128)S(1)} %subtract_convert_fusion.10, ...), kind=kOutput, calls=%fused_computation.15.clone.1 | convolution fusion | flops 1662517248 | bytes 34406432 | tf_op jit(solution)/shard_map/while/body/eval_jaxpr/vmap(hqk,qhd->khd)/dot_general | solution.py:272
  574.0 13.2 %fusion.215 = bf16[2,8,768,64]{2,3,1,0:T(8,128)(2,1)S(1)} fusion(bf16[2,512,8,64]{1,3,2,0:T(8,128)(2,1)} %get-tuple-element.2053, f32[2,8,768,512]{3,2,1,0:T(8,128)} %fusion.214, f32[2,8,512]{2,1,0:T(8,128)} %get-tuple-element.2052, f32[2,512,768]{1,2,0:T(8,128)S(1)} %subtract_convert_fusion.10, f32[8]{0:T(128)} %get-tuple-element.2050, ...), kind=kOutput, calls=%fused_computation.10.clone.1 | convolution fusion | flops 843055104 | bytes 31752224 | tf_op jit(solution)/shard_map/while/body/eval_jaxpr/vmap(hqk,qhd->khd)/dot_general | solution.py:265
  605.4 4.7 convolution_bitcast_fusion.2
  610.0 61.7 %reduce-scatter.2.cloned.1.call-done = bf16[768,2,1024]{2,0,1:T(8,128)(2,1)} async-done(((bf16[1536,2,1024]{2,0,1:T(8,128)(2,1)}), bf16[768,2,1024]{2,0,1:T(8,128)(2,1)}) %reduce-scatter.2.cloned.1.call-update) | async-done | bytes 3145744 | tf_op jit(solution)/shard_map/reduce_scatter | solution.py:296
  678.1 6.3 add_convert_fusion.2
  690.5 41.0 %all-reduce = (f32[512]{0:T(512)}, f32[512]{0:T(512)}, f32[8]{0:T(128)}, f32[512]{0:T(512)}, f32[512]{0:T(512)}) all-reduce(f32[512]{0:T(512)S(1)} %add.197, f32[512]{0:T(512)S(1)} %add.198, f32[8]{0:T(128)S(1)} %reduce_sum.201, f32[512]{0:T(512)S(1)} %copy-done.65, ...), channel_id=1, replica_groups=mesh['seq'=16,'blk'=2] {'seq','blk'}, use_global_device_ids=true, to_apply=%region_31.32 | all-reduce | flops 2056 | bytes 16448 | tf_op jit(solution)/shard_map/psum | solution.py:328
  734.8 183.1 %all-reduce.4.cloned.1.call-done = (f32[512,512]{1,0:T(8,128)}, f32[512,512]{1,0:T(8,128)}, f32[512,512]{1,0:T(8,128)}, f32[512,512]{1,0:T(8,128)}, f32[512,2048]{1,0:T(8,128)}, /*index=5*/f32[2048,512]{1,0:T(8,128)}) async-done(((f32[512,512]{1,0:T(8,128)}, f32[512,512]{1,0:T(8,128)}, f32[512,512]{1,0:T(8,128)}, f32[512,512]{1,0:T(8,128)}, f32[512,2048]{1,0:T(8,128)}, /*index=5*/f32[2048,512]{1,0:T(8,128)}), ...) | async-done | bytes 12582928 | tf_op jit(solution)/shard_map/psum | solution.py:328
  (440 shorter events, 280.6 us)
Async XLA Ops:
  7.2 274.5 %copy-start = (bf16[512,2048]{1,0:T(8,128)(2,1)S(1)}, bf16[512,2048]{1,0:T(8,128)(2,1)}, u32[]{:S(2)}) copy-start(bf16[512,2048]{1,0:T(8,128)(2,1)} %param.47) | copy-start | bytes 6291460
  7.2 12.1 %copy-start.2 = (bf16[2,512,512]{2,1,0:T(8,128)(2,1)S(1)}, bf16[2,512,512]{2,1,0:T(8,128)(2,1)}, u32[]{:S(2)}) copy-start(bf16[2,512,512]{2,1,0:T(8,128)(2,1)} %param.32) | copy-start | bytes 3145732
  7.2 10.6 %copy-start.48 = (f32[512]{0:T(512)S(1)}, f32[512]{0:T(512)}, u32[]{:S(2)}) copy-start(f32[512]{0:T(512)} %param.38) | copy-start | bytes 6148
  7.2 10.6 %copy-start.63 = (f32[512]{0:T(512)S(1)}, f32[512]{0:T(512)}, u32[]{:S(2)}) copy-start(f32[512]{0:T(512)} %param.39) | copy-start | bytes 6148
  7.2 100.6 %all-gather.2.cloned.1.call-start = ((), (), s32[]{:S(2)}) async-start(), calls=%async_computation.1 | async-start | bytes 9437184 | tf_op jit(solution)/shard_map/all_gather | solution.py:85
  8.6 11.1 %copy-start.56 = (f32[2,256]{1,0:T(2,128)}, f32[2,256]{1,0:T(2,128)S(1)}, u32[]{:S(2)}) copy-start(f32[2,256]{1,0:T(2,128)S(1)} %broadcast_multiply_fusion.2) | copy-start | bytes 6148
  10.0 9.8 %copy-start.61 = (f32[2,256]{1,0:T(2,128)}, f32[2,256]{1,0:T(2,128)S(1)}, u32[]{:S(2)}) copy-start(f32[2,256]{1,0:T(2,128)S(1)} %add_rsqrt_fusion) | copy-start | bytes 6148
  11.5 8.3 copy-start.38
  13.7 10.8 %copy-start.44 = (f32[2,512]{1,0:T(2,128)}, f32[2,512]{1,0:T(2,128)S(1)}, u32[]{:S(2)}) copy-start(f32[2,512]{1,0:T(2,128)S(1)} %fusion.125) | copy-start | bytes 12292
  24.5 6.9 copy-start.28
  24.6 647.1 %reduce-scatter.2.cloned.1.call-start = ((), (), s32[]{:S(2)}) async-start(), calls=%async_computation.2 | async-start | bytes 9437184 | tf_op jit(solution)/shard_map/reduce_scatter | solution.py:296
  160.9 6.7 copy-start.8
  176.6 6.7 copy-start.8
  244.9 6.7 copy-start.8
  260.6 6.7 copy-start.8
  281.2 35.2 %copy-start.4 = (f32[2,512,512]{2,1,0:T(8,128)}, f32[2,512,512]{2,1,0:T(8,128)S(1)}, u32[]{:S(2)}) copy-start(f32[2,512,512]{2,1,0:T(8,128)S(1)} %get-tuple-element.1057) | copy-start | bytes 6291460
  281.2 35.2 %copy-start.40 = (f32[2,512]{1,0:T(2,128)}, f32[2,512]{1,0:T(2,128)S(1)}, u32[]{:S(2)}) copy-start(f32[2,512]{1,0:T(2,128)S(1)} %broadcast_multiply_fusion) | copy-start | bytes 12292
  281.7 34.7 %copy-start.42 = (f32[2,512]{1,0:T(2,128)}, f32[2,512]{1,0:T(2,128)S(1)}, u32[]{:S(2)}) copy-start(f32[2,512]{1,0:T(2,128)S(1)} %fusion.126) | copy-start | bytes 12292
  285.9 20.2 %copy-start.23 = (bf16[2,512,512]{2,1,0:T(8,128)(2,1)S(1)}, bf16[2,512,512]{2,1,0:T(8,128)(2,1)}, u32[]{:S(2)}) copy-start(bf16[2,512,512]{2,1,0:T(8,128)(2,1)} %param.49) | copy-start | bytes 3145732
  285.9 20.2 %copy-start.72 = (bf16[2048,512]{1,0:T(8,128)(2,1)S(1)}, bf16[2048,512]{1,0:T(8,128)(2,1)}, u32[]{:S(2)}) copy-start(bf16[2048,512]{1,0:T(8,128)(2,1)} %param.48) | copy-start | bytes 6291460
  312.9 3.4 copy-start.15
  376.2 23.1 %copy-start.67 = (f32[2,8]{1,0:T(2,128)S(1)}, f32[2,8]{1,0:T(2,128)}, u32[]{:S(2)}) copy-start(f32[2,8]{1,0:T(2,128)} %get-tuple-element.1969) | copy-start | bytes 196 | tf_op jit(solution)/shard_map/while
  376.2 23.1 %copy-start.58 = (f32[2,8,512]{2,1,0:T(8,128)S(1)}, f32[2,8,512]{2,1,0:T(8,128)}, u32[]{:S(2)}) copy-start(f32[2,8,512]{2,1,0:T(8,128)} %get-tuple-element.1968) | copy-start | bytes 98308 | tf_op jit(solution)/shard_map/while
  453.6 23.1 %copy-start.67 = (f32[2,8]{1,0:T(2,128)S(1)}, f32[2,8]{1,0:T(2,128)}, u32[]{:S(2)}) copy-start(f32[2,8]{1,0:T(2,128)} %get-tuple-element.1969) | copy-start | bytes 196 | tf_op jit(solution)/shard_map/while
  453.6 23.1 %copy-start.58 = (f32[2,8,512]{2,1,0:T(8,128)S(1)}, f32[2,8,512]{2,1,0:T(8,128)}, u32[]{:S(2)}) copy-start(f32[2,8,512]{2,1,0:T(8,128)} %get-tuple-element.1968) | copy-start | bytes 98308 | tf_op jit(solution)/shard_map/while
  485.4 11.3 %copy-start.60 = (f32[2,8,512]{2,1,0:T(8,128)S(1)}, f32[2,8,512]{2,1,0:T(8,128)}, u32[]{:S(2)}) copy-start(f32[2,8,512]{2,1,0:T(8,128)} %get-tuple-element.2054) | copy-start | bytes 98308 | tf_op jit(solution)/shard_map/while
  515.8 13.2 %copy-start.7 = (bf16[2,8,768,64]{2,3,1,0:T(8,128)(2,1)S(1)}, bf16[2,8,768,64]{2,3,1,0:T(8,128)(2,1)}, u32[]{:S(2)}) copy-start(bf16[2,8,768,64]{2,3,1,0:T(8,128)(2,1)} %fusion.216) | copy-start | bytes 4718596 | tf_op jit(solution)/shard_map/while
  543.7 11.3 %copy-start.60 = (f32[2,8,512]{2,1,0:T(8,128)S(1)}, f32[2,8,512]{2,1,0:T(8,128)}, u32[]{:S(2)}) copy-start(f32[2,8,512]{2,1,0:T(8,128)} %get-tuple-element.2054) | copy-start | bytes 98308 | tf_op jit(solution)/shard_map/while
  574.0 13.2 %copy-start.7 = (bf16[2,8,768,64]{2,3,1,0:T(8,128)(2,1)S(1)}, bf16[2,8,768,64]{2,3,1,0:T(8,128)(2,1)}, u32[]{:S(2)}) copy-start(bf16[2,8,768,64]{2,3,1,0:T(8,128)(2,1)} %fusion.216) | copy-start | bytes 4718596 | tf_op jit(solution)/shard_map/while
  594.5 323.4 %all-reduce.4.cloned.1.call-start = ((), (), s32[]{:S(2)}) async-start(), calls=%async_computation.3 | async-start | bytes 25165824 | tf_op jit(solution)/shard_map/psum | solution.py:328
  596.0 4.9 copy-start.22
  596.0 4.9 copy-start.24
  600.9 4.5 copy-start.5
  600.9 4.5 copy-start.16
  600.9 4.5 copy-start.41
  600.9 4.5 copy-start.43
  600.9 4.5 copy-start.47
  600.9 4.5 copy-start.55
  678.1 6.3 copy-start.33
  678.1 6.3 copy-start.35
  678.1 6.3 copy-start.71
  687.9 43.6 %copy-start.11 = (f32[2,512,512]{2,1,0:T(8,128)S(1)}, f32[2,512,512]{2,1,0:T(8,128)}, u32[]{:S(2)}) copy-start(f32[2,512,512]{2,1,0:T(8,128)} %copy-done.10) | copy-start | bytes 6291460
  687.9 43.6 %copy-start.51 = (f32[2,512]{1,0:T(2,128)S(1)}, f32[2,512]{1,0:T(2,128)}, u32[]{:S(2)}) copy-start(f32[2,512]{1,0:T(2,128)} %copy-done.50) | copy-start | bytes 12292
  917.9 4.8 copy-start.30
  917.9 5.8 copy-start.29
  920.3 4.4 copy-start.19
  924.7 3.7 copy-start.18
  924.7 5.7 copy-start.1
  (50 other events, 88.1 us)
Sparse Core Ops, SparseCore 0:
  24.7 83.0 all-gather.1
  594.6 77.0 reduce-scatter.1
  680.4 237.4 all-reduce.3
where the time goes:
time: 945 us; the launch traced here: 937 us
  waiting for transfers between devices  318 us (34%)
  matrix products  271 us (29%)
  local copies, waits for them, and re-layouts  199 us (21%)
  other arithmetic  75.8 us (8%)
  blocking collectives  46.4 us (5%)
  between operations  14.8 us (2%)
  loops' own time  11.7 us (1%)
    psum x1, waiting for transfers between devices, per_device(): lax.psum((grad_first_g, grad_first_b, grad_query_w, grad_key_w, grad_valu...  183 us
    all_gather x1, waiting for transfers between devices, per_device(): lax.all_gather(key_value, 'blk', axis=0, tiled=True)  73.6 us
    reduce_scatter x1, waiting for transfers between devices, per_device(): lax.psum_scatter(pieces.reshape(lax.axis_size('blk') * key_rows, seq_coun...  61.7 us
    dot_general x14, matrix products, block_scores(): jnp.einsum('qhd,khd->hqk', q_heads, key_block, preferred_element_type=jnp...  58.7 us
    dot_general x8, matrix products, probs_of(): jnp.einsum('qhd,khd->hqk', d_heads, value_block, preferred_element_type=j...  57.9 us
    psum x1, blocking collectives, per_device(): lax.psum((grad_first_g, grad_first_b, grad_query_w, grad_key_w, grad_valu...  41 us
    dot_general x2, matrix products, pair_terms(): jnp.einsum('hqk,qhd->khd', d_scores, q_heads, preferred_element_type=jnp....  38 us
    dot_general x4, matrix products, out_step(): jnp.einsum('hqk,khd->qhd', attn_probs, pieces[3], preferred_element_type=...  32.2 us
  transfers between devices with their start and end apart: 3, of which 3 were waited for; matrix products, arithmetic and copies ran while one was open for 3% of the time, Pallas kernels for 0%

commit v1 on v0

--- a/solution.py
+++ b/solution.py
@@ -6,6 +6,11 @@
 
 epsilon = 1e-05
 far_order = 1073741824
+
+
+def tell_set(chunk, row_axis, shard_axis="seq"):
+    far_arr = lax.psum(chunk, row_axis)
+    return lax.psum(far_arr, shard_axis)
 
 
 def layer_norm(values, gain, shift):
@@ -325,7 +330,7 @@
     input_grad = (d_tokens + d_residual).astype(jnp.bfloat16)
     grad_first_g = gain_slots + gain_mem
     grad_first_b = shift_slots + shift_mem
-    summed = lax.psum(
+    summed = tell_set(
         (
             grad_first_g,
             grad_first_b,
@@ -339,7 +344,7 @@
             grad_hidden_w,
             grad_output_w,
         ),
-        ("seq", "blk"),
+        "blk",
     )
     return (
         layer_out,

time: 945 us -> 1240 us (1.31)
  waiting for transfers between devices: 318 us -> 611 us
    psum x1 -> x2, waiting for transfers between devices: 183 us -> 476 us  [the longest x1 292 us: tell_set(): far_arr = lax.psum(chunk, row_axis)]
    psum x1 -> x2, blocking collectives: 41 us -> 42.4 us  [the longest x1 37.4 us: tell_set(): return lax.psum(far_arr, shard_axis)]
  transfers between devices with their start and end apart: 3 -> 4, of which waited for: 3 -> 4; matrix products, arithmetic and copies ran while one was open for 3% -> 3% of each run, Pallas kernels for 0% -> 0%
where the time goes in v1:
time: 1240 us; the launch traced here: 1230 us
  waiting for transfers between devices  611 us (49%)
  matrix products  271 us (22%)
  local copies, waits for them, and re-layouts  199 us (16%)
  other arithmetic  75.8 us (6%)
  blocking collectives  47.8 us (4%)
  between operations  14.8 us (1%)
    psum x1, waiting for transfers between devices, tell_set(): far_arr = lax.psum(chunk, row_axis)  292 us
    psum x1, waiting for transfers between devices, tell_set(): return lax.psum(far_arr, shard_axis)  184 us
    all_gather x1, waiting for transfers between devices, per_device(): lax.all_gather(key_value, 'blk', axis=0, tiled=True)  73.6 us
    reduce_scatter x1, waiting for transfers between devices, per_device(): lax.psum_scatter(pieces.reshape(lax.axis_size('blk') * key_rows, seq_coun...  61.7 us
    dot_general x14, matrix products, block_scores(): jnp.einsum('qhd,khd->hqk', q_heads, key_block, preferred_element_type=jnp...  58.7 us
    dot_general x8, matrix products, probs_of(): jnp.einsum('qhd,khd->hqk', d_heads, value_block, preferred_element_type=j...  57.9 us
    dot_general x2, matrix products, pair_terms(): jnp.einsum('hqk,qhd->khd', d_scores, q_heads, preferred_element_type=jnp....  38 us
    psum x1, blocking collectives, tell_set(): return lax.psum(far_arr, shard_axis)  37.4 us
  transfers between devices with their start and end apart: 4, of which 4 were waited for; matrix products, arithmetic and copies ran while one was open for 3% of the time, Pallas kernels for 0%

profile of v1, /device:TPU:0, one launch (start us, length us, event | category | flops | bytes accessed | tf_op | source)
XLA Modules:
  0.0 1231.6 jit_solution(710226211708778304)
XLA Ops:
  26.0 5.4 all_gather.7
  34.2 73.6 %all-gather.2.cloned.1.call-done = bf16[1536,2,1024]{0,2,1:T(8,128)(2,1)} async-done(((bf16[768,2,1024]{0,2,1:T(8,128)(2,1)}), bf16[1536,2,1024]{0,2,1:T(8,128)(2,1)}) %all-gather.2.cloned.1.call-update) | async-done | bytes 6291472 | tf_op jit(solution)/shard_map/all_gather | solution.py:90
  110.0 168.7 %while.93 = (s32[]{:T(128)}, bf16[2,512,8,64]{1,3,2,0:T(8,128)(2,1)}, f32[2,8,512]{2,1,0:T(8,128)}, s32[2]{0:T(128)}, bf16[1536,2,1024]{0,2,1:T(8,128)(2,1)}, /*...) while((s32[]{:T(128)}, ...), condition=%wide.region_11.12_spmd.clone, body=%wide.region_4.11_spmd.clone.sunk | while | flops 1264345600 | bytes 82579288 | solution.py:161
  138.4 21.8 %while.98 = (s32[]{:T(128)}, f32[8,512]{1,0:T(8,128)S(1)}, f32[8,512]{1,0:T(8,128)S(1)}, s32[2,768]{1,0:T(2,128)S(1)}, s32[512]{0:T(512)S(1)}, /*index=5*/bf16[2...) while((s32[]{:T(128)}, f32[8,512]{1,0:T(8,128)S(1)}, ...), condition=%wide.region_8.8_spmd.clone, body=%wide.region_5.7_spmd.clone.sunk | while | flops 438456320 | bytes 32610988 | solution.py:130
  139.6 5.3 fusion.232
  150.5 5.3 fusion.232
  160.9 31.5 %while.99 = (s32[]{:T(128)}, f32[512,8,64]{0,2,1:T(8,128)}, bf16[2,768,8,64]{1,3,2,0:T(8,128)(2,1)}, s32[2,768]{1,0:T(2,128)S(1)}, s32[512]{0:T(512)S(1)}, /*ind...) while((s32[]{:T(128)}, f32[512,8,64]{0,2,1:T(8,128)}, ...), condition=%wide.region_10.10_spmd.clone, body=%wide.region_9.9_spmd.clone.sunk | while | flops 825884672 | bytes 19438292 | solution.py:156
  167.6 8.0 fusion.238
  183.4 8.1 fusion.238
  222.5 21.8 %while.98 = (s32[]{:T(128)}, f32[8,512]{1,0:T(8,128)S(1)}, f32[8,512]{1,0:T(8,128)S(1)}, s32[2,768]{1,0:T(2,128)S(1)}, s32[512]{0:T(512)S(1)}, /*index=5*/bf16[2...) while((s32[]{:T(128)}, f32[8,512]{1,0:T(8,128)S(1)}, ...), condition=%wide.region_8.8_spmd.clone, body=%wide.region_5.7_spmd.clone.sunk | while | flops 438456320 | bytes 32610988 | solution.py:130
  223.7 5.3 fusion.232
  234.5 5.3 fusion.232
  244.9 31.5 %while.99 = (s32[]{:T(128)}, f32[512,8,64]{0,2,1:T(8,128)}, bf16[2,768,8,64]{1,3,2,0:T(8,128)(2,1)}, s32[2,768]{1,0:T(2,128)S(1)}, s32[512]{0:T(512)S(1)}, /*ind...) while((s32[]{:T(128)}, f32[512,8,64]{0,2,1:T(8,128)}, ...), condition=%wide.region_10.10_spmd.clone, body=%wide.region_9.9_spmd.clone.sunk | while | flops 825884672 | bytes 19438292 | solution.py:156
  251.6 8.1 fusion.238
  267.4 8.1 fusion.238
  286.0 20.1 %multiply_convert_fusion = (bf16[2,512,2048]{2,1,0:T(8,128)(2,1)}, f32[2,512,2048]{2,1,0:T(8,128)}) fusion(f32[2,512,2048]{2,1,0:T(8,128)S(1)} %get-tuple-element.1069, u8[512,2048]{1,0:T(8,128)(4,1)S(1)} %get-tuple-element.841, u8[512,2048]{1,0:T(8,128)(4,1)S(1)} %get-tuple-element.840), kind=kLoop, calls=%fused_computation.134 | loop fusion | flops 146800640 | bytes 23068672 | tf_op jit(solution)/shard_map/convert_element_type | solution.py:170
  306.1 6.8 add_convert_fusion
  322.6 155.2 %while.96 = (s32[]{:T(128)}, bf16[2,512,8,64]{1,3,2,0:T(8,128)(2,1)}, f32[2,8,512]{2,1,0:T(8,128)}, f32[2,8]{1,0:T(2,128)}, s32[2]{0:T(128)}, /*index=5*/bf16[15...) while((s32[]{:T(128)}, ...), condition=%wide.region_23.24_spmd.clone, body=%wide.region_16.23_spmd.clone.sunk | while | flops 2073039360 | bytes 125587736 | solution.py:253
  334.2 4.7 copy.151
  348.6 5.2 reshape.456
  358.2 18.1 %while.100 = (s32[]{:T(128)}, f32[8,512]{1,0:T(8,128)S(1)}, s32[2,768]{1,0:T(2,128)S(1)}, s32[512]{0:T(512)S(1)}, bf16[2,768,8,64]{1,3,2,0:T(8,128)(2,1)S(1)}, /...) while((s32[]{:T(128)}, f32[8,512]{1,0:T(8,128)S(1)}, ...), condition=%wide.region_19.19_spmd.clone, body=%wide.region_17.18_spmd.clone.sunk | while | flops 828510208 | bytes 40212728 | solution.py:227
  360.5 6.6 fusion.222
  369.6 6.6 fusion.222
  376.3 23.0 %while.101 = (s32[]{:T(128)}, f32[512,8,64]{0,2,1:T(8,128)S(1)}, f32[8]{0:T(128)S(1)}, bf16[2,768,8,64]{1,3,2,0:T(8,128)(2,1)S(1)}, s32[2,768]{1,0:T(2,128)S(1)}...) while((s32[]{:T(128)}, f32[512,8,64]{0,2,1:T(8,128)S(1)}, ...), condition=%wide.region_22.22_spmd.clone, body=%wide.region_20.21_spmd.clone.sunk | while | flops 1244266496 | bytes 49339216 | solution.py:248
  378.6 7.8 multiply_reduce_fusion.5
  390.1 7.8 multiply_reduce_fusion.5
  411.6 4.7 copy.151
  425.9 5.2 reshape.456
  435.5 18.1 %while.100 = (s32[]{:T(128)}, f32[8,512]{1,0:T(8,128)S(1)}, s32[2,768]{1,0:T(2,128)S(1)}, s32[512]{0:T(512)S(1)}, bf16[2,768,8,64]{1,3,2,0:T(8,128)(2,1)S(1)}, /...) while((s32[]{:T(128)}, f32[8,512]{1,0:T(8,128)S(1)}, ...), condition=%wide.region_19.19_spmd.clone, body=%wide.region_17.18_spmd.clone.sunk | while | flops 828510208 | bytes 40212728 | solution.py:227
  437.9 6.6 fusion.222
  446.9 6.6 fusion.222
  453.6 23.0 %while.101 = (s32[]{:T(128)}, f32[512,8,64]{0,2,1:T(8,128)S(1)}, f32[8]{0:T(128)S(1)}, bf16[2,768,8,64]{1,3,2,0:T(8,128)(2,1)S(1)}, s32[2,768]{1,0:T(2,128)S(1)}...) while((s32[]{:T(128)}, f32[512,8,64]{0,2,1:T(8,128)S(1)}, ...), condition=%wide.region_22.22_spmd.clone, body=%wide.region_20.21_spmd.clone.sunk | while | flops 1244266496 | bytes 49339216 | solution.py:248
  456.0 7.8 multiply_reduce_fusion.5
  467.5 7.8 multiply_reduce_fusion.5
  477.8 116.6 %while.97 = (s32[]{:T(128)}, bf16[2,768,2,1024]{3,1,0,2:T(8,128)(2,1)}, s32[2]{0:T(128)S(1)}, s32[2,2,1536]{2,1,0:T(2,128)}, bf16[1536,2,1024]{0,2,1:T(8,128)(2,...) while((s32[]{:T(128)}, ...), condition=%wide.region_25.26_spmd.clone, body=%wide.region_24.25_spmd.clone.sunk | while | flops 3319529984 | bytes 129511832 | solution.py:300
  485.4 11.3 fusion.214
  496.8 19.0 %fusion.216 = bf16[2,8,768,64]{2,3,1,0:T(8,128)(2,1)} fusion(bf16[2,512,8,64]{1,3,2,0:T(8,128)(2,1)} %get-tuple-element.2060, f32[2,8,768,512]{3,2,1,0:T(8,128)} %fusion.214, f32[2,8,512]{2,1,0:T(8,128)S(1)} %copy-done.60, f32[2,8,512]{2,1,0:T(8,128)} %get-tuple-element.2063, f32[2,512,768]{1,2,0:T(8,128)S(1)} %subtract_convert_fusion.10, ...), kind=kOutput, calls=%fused_computation.15.clone.1 | convolution fusion | flops 1662517248 | bytes 34406432 | tf_op jit(solution)/shard_map/while/body/eval_jaxpr/vmap(hqk,qhd->khd)/dot_general | solution.py:277
  515.8 13.2 %fusion.215 = bf16[2,8,768,64]{2,3,1,0:T(8,128)(2,1)S(1)} fusion(bf16[2,512,8,64]{1,3,2,0:T(8,128)(2,1)} %get-tuple-element.2064, f32[2,8,768,512]{3,2,1,0:T(8,128)} %fusion.214, f32[2,8,512]{2,1,0:T(8,128)} %get-tuple-element.2063, f32[2,512,768]{1,2,0:T(8,128)S(1)} %subtract_convert_fusion.10, f32[8]{0:T(128)} %get-tuple-element.2061, ...), kind=kOutput, calls=%fused_computation.10.clone.1 | convolution fusion | flops 843055104 | bytes 31752224 | tf_op jit(solution)/shard_map/while/body/eval_jaxpr/vmap(hqk,qhd->khd)/dot_general | solution.py:270
  543.7 11.3 fusion.214
  555.0 19.0 %fusion.216 = bf16[2,8,768,64]{2,3,1,0:T(8,128)(2,1)} fusion(bf16[2,512,8,64]{1,3,2,0:T(8,128)(2,1)} %get-tuple-element.2060, f32[2,8,768,512]{3,2,1,0:T(8,128)} %fusion.214, f32[2,8,512]{2,1,0:T(8,128)S(1)} %copy-done.60, f32[2,8,512]{2,1,0:T(8,128)} %get-tuple-element.2063, f32[2,512,768]{1,2,0:T(8,128)S(1)} %subtract_convert_fusion.10, ...), kind=kOutput, calls=%fused_computation.15.clone.1 | convolution fusion | flops 1662517248 | bytes 34406432 | tf_op jit(solution)/shard_map/while/body/eval_jaxpr/vmap(hqk,qhd->khd)/dot_general | solution.py:277
  574.0 13.2 %fusion.215 = bf16[2,8,768,64]{2,3,1,0:T(8,128)(2,1)S(1)} fusion(bf16[2,512,8,64]{1,3,2,0:T(8,128)(2,1)} %get-tuple-element.2064, f32[2,8,768,512]{3,2,1,0:T(8,128)} %fusion.214, f32[2,8,512]{2,1,0:T(8,128)} %get-tuple-element.2063, f32[2,512,768]{1,2,0:T(8,128)S(1)} %subtract_convert_fusion.10, f32[8]{0:T(128)} %get-tuple-element.2061, ...), kind=kOutput, calls=%fused_computation.10.clone.1 | convolution fusion | flops 843055104 | bytes 31752224 | tf_op jit(solution)/shard_map/while/body/eval_jaxpr/vmap(hqk,qhd->khd)/dot_general | solution.py:270
  605.4 4.7 convolution_bitcast_fusion.2
  610.0 61.7 %reduce-scatter.2.cloned.1.call-done = bf16[768,2,1024]{2,0,1:T(8,128)(2,1)} async-done(((bf16[1536,2,1024]{2,0,1:T(8,128)(2,1)}), bf16[768,2,1024]{2,0,1:T(8,128)(2,1)}) %reduce-scatter.2.cloned.1.call-update) | async-done | bytes 3145744 | tf_op jit(solution)/shard_map/reduce_scatter | solution.py:301
  677.4 291.6 %all-reduce.9.cloned.1.call-done = (f32[512,512]{1,0:T(8,128)}, f32[512,512]{1,0:T(8,128)}, f32[512,512]{1,0:T(8,128)}, f32[512,512]{1,0:T(8,128)}, f32[512,2048]{1,0:T(8,128)}, /*index=5*/f32[2048,512]{1,0:T(8,128)}) async-done(((f32[512,512]{1,0:T(8,128)}, f32[512,512]{1,0:T(8,128)}, f32[512,512]{1,0:T(8,128)}, f32[512,512]{1,0:T(8,128)}, f32[512,2048]{1,0:T(8,128)}, /*index=5*/f32[2048,512]{1,0:T(8,128)}), ...) | async-done | bytes 12582928 | tf_op jit(solution)/shard_map/psum | solution.py:12
  969.8 6.3 add_convert_fusion.2
  982.2 5.1 all-reduce.2
  987.2 37.4 %all-reduce = (f32[512]{0:T(512)}, f32[512]{0:T(512)}, f32[8]{0:T(128)}, f32[512]{0:T(512)}, f32[512]{0:T(512)}) all-reduce(f32[512]{0:T(512)S(1)} %get-tuple-element.1026, f32[512]{0:T(512)S(1)} %get-tuple-element.1027, f32[8]{0:T(128)S(1)} %get-tuple-element.1028, ...), channel_id=1, replica_groups=mesh['seq'=16,'blk'=2] {'seq'}, use_global_device_ids=true, to_apply=%region_32.33 | all-reduce | flops 2056 | bytes 16448 | tf_op jit(solution)/shard_map/psum | solution.py:13
  1027.9 184.5 %all-reduce.7.cloned.1.call-done = (f32[512,512]{1,0:T(8,128)}, f32[512,512]{1,0:T(8,128)}, f32[512,512]{1,0:T(8,128)}, f32[512,512]{1,0:T(8,128)}, f32[512,2048]{1,0:T(8,128)}, /*index=5*/f32[2048,512]{1,0:T(8,128)}) async-done(((f32[512,512]{1,0:T(8,128)}, f32[512,512]{1,0:T(8,128)}, f32[512,512]{1,0:T(8,128)}, f32[512,512]{1,0:T(8,128)}, f32[512,2048]{1,0:T(8,128)}, /*index=5*/f32[2048,512]{1,0:T(8,128)}), ...) | async-done | bytes 12582928 | tf_op jit(solution)/shard_map/psum | solution.py:13
  (444 shorter events, 289.9 us)
Async XLA Ops:
  7.2 274.5 %copy-start = (bf16[512,2048]{1,0:T(8,128)(2,1)S(1)}, bf16[512,2048]{1,0:T(8,128)(2,1)}, u32[]{:S(2)}) copy-start(bf16[512,2048]{1,0:T(8,128)(2,1)} %param.47) | copy-start | bytes 6291460
  7.2 12.1 copy-start.2
  7.2 10.6 copy-start.48
  7.2 10.6 copy-start.63
  7.2 100.6 %all-gather.2.cloned.1.call-start = ((), (), s32[]{:S(2)}) async-start(), calls=%async_computation.1 | async-start | bytes 9437184 | tf_op jit(solution)/shard_map/all_gather | solution.py:90
  8.6 11.1 copy-start.56
  10.0 9.8 copy-start.61
  11.5 8.3 copy-start.38
  13.7 10.8 copy-start.44
  24.5 6.9 copy-start.28
  24.6 647.1 %reduce-scatter.2.cloned.1.call-start = ((), (), s32[]{:S(2)}) async-start(), calls=%async_computation.2 | async-start | bytes 9437184 | tf_op jit(solution)/shard_map/reduce_scatter | solution.py:301
  160.9 6.7 copy-start.8
  176.6 6.7 copy-start.8
  244.9 6.7 copy-start.8
  260.6 6.7 copy-start.8
  281.2 35.2 %copy-start.4 = (f32[2,512,512]{2,1,0:T(8,128)}, f32[2,512,512]{2,1,0:T(8,128)S(1)}, u32[]{:S(2)}) copy-start(f32[2,512,512]{2,1,0:T(8,128)S(1)} %get-tuple-element.1068) | copy-start | bytes 6291460
  281.2 35.2 %copy-start.40 = (f32[2,512]{1,0:T(2,128)}, f32[2,512]{1,0:T(2,128)S(1)}, u32[]{:S(2)}) copy-start(f32[2,512]{1,0:T(2,128)S(1)} %broadcast_multiply_fusion) | copy-start | bytes 12292
  281.7 34.7 %copy-start.42 = (f32[2,512]{1,0:T(2,128)}, f32[2,512]{1,0:T(2,128)S(1)}, u32[]{:S(2)}) copy-start(f32[2,512]{1,0:T(2,128)S(1)} %fusion.126) | copy-start | bytes 12292
  285.9 20.2 %copy-start.23 = (bf16[2,512,512]{2,1,0:T(8,128)(2,1)S(1)}, bf16[2,512,512]{2,1,0:T(8,128)(2,1)}, u32[]{:S(2)}) copy-start(bf16[2,512,512]{2,1,0:T(8,128)(2,1)} %param.49) | copy-start | bytes 3145732
  285.9 20.2 %copy-start.72 = (bf16[2048,512]{1,0:T(8,128)(2,1)S(1)}, bf16[2048,512]{1,0:T(8,128)(2,1)}, u32[]{:S(2)}) copy-start(bf16[2048,512]{1,0:T(8,128)(2,1)} %param.48) | copy-start | bytes 6291460
  376.2 23.1 %copy-start.67 = (f32[2,8]{1,0:T(2,128)S(1)}, f32[2,8]{1,0:T(2,128)}, u32[]{:S(2)}) copy-start(f32[2,8]{1,0:T(2,128)} %get-tuple-element.1980) | copy-start | bytes 196 | tf_op jit(solution)/shard_map/while
  376.2 23.1 %copy-start.58 = (f32[2,8,512]{2,1,0:T(8,128)S(1)}, f32[2,8,512]{2,1,0:T(8,128)}, u32[]{:S(2)}) copy-start(f32[2,8,512]{2,1,0:T(8,128)} %get-tuple-element.1979) | copy-start | bytes 98308 | tf_op jit(solution)/shard_map/while
  453.6 23.1 %copy-start.67 = (f32[2,8]{1,0:T(2,128)S(1)}, f32[2,8]{1,0:T(2,128)}, u32[]{:S(2)}) copy-start(f32[2,8]{1,0:T(2,128)} %get-tuple-element.1980) | copy-start | bytes 196 | tf_op jit(solution)/shard_map/while
  453.6 23.1 %copy-start.58 = (f32[2,8,512]{2,1,0:T(8,128)S(1)}, f32[2,8,512]{2,1,0:T(8,128)}, u32[]{:S(2)}) copy-start(f32[2,8,512]{2,1,0:T(8,128)} %get-tuple-element.1979) | copy-start | bytes 98308 | tf_op jit(solution)/shard_map/while
  485.4 11.3 copy-start.60
  515.8 13.2 %copy-start.7 = (bf16[2,8,768,64]{2,3,1,0:T(8,128)(2,1)S(1)}, bf16[2,8,768,64]{2,3,1,0:T(8,128)(2,1)}, u32[]{:S(2)}) copy-start(bf16[2,8,768,64]{2,3,1,0:T(8,128)(2,1)} %fusion.216) | copy-start | bytes 4718596 | tf_op jit(solution)/shard_map/while
  543.7 11.3 copy-start.60
  574.0 13.2 %copy-start.7 = (bf16[2,8,768,64]{2,3,1,0:T(8,128)(2,1)S(1)}, bf16[2,8,768,64]{2,3,1,0:T(8,128)(2,1)}, u32[]{:S(2)}) copy-start(bf16[2,8,768,64]{2,3,1,0:T(8,128)(2,1)} %fusion.216) | copy-start | bytes 4718596 | tf_op jit(solution)/shard_map/while
  594.5 374.6 %all-reduce.9.cloned.1.call-start = ((), (), s32[]{:S(2)}) async-start(), calls=%async_computation.4 | async-start | bytes 25165824 | tf_op jit(solution)/shard_map/psum | solution.py:12
  596.0 4.9 copy-start.22
  596.0 4.9 copy-start.24
  600.9 4.5 copy-start.5
  600.9 4.5 copy-start.16
  600.9 4.5 copy-start.41
  600.9 4.5 copy-start.43
  600.9 4.5 copy-start.47
  600.9 4.5 copy-start.55
  677.4 535.0 %all-reduce.7.cloned.1.call-start = ((), (), s32[]{:S(2)}) async-start(), calls=%async_computation.3 | async-start | bytes 25165824 | tf_op jit(solution)/shard_map/psum | solution.py:13
  969.8 6.3 copy-start.33
  969.8 6.3 copy-start.35
  969.8 6.3 copy-start.71
  979.6 45.0 %copy-start.11 = (f32[2,512,512]{2,1,0:T(8,128)S(1)}, f32[2,512,512]{2,1,0:T(8,128)}, u32[]{:S(2)}) copy-start(f32[2,512,512]{2,1,0:T(8,128)} %copy-done.10) | copy-start | bytes 6291460
  979.7 45.0 %copy-start.51 = (f32[2,512]{1,0:T(2,128)S(1)}, f32[2,512]{1,0:T(2,128)}, u32[]{:S(2)}) copy-start(f32[2,512]{1,0:T(2,128)} %copy-done.50) | copy-start | bytes 12292
  1212.4 4.8 copy-start.30
  1212.4 5.8 copy-start.29
  1214.8 4.4 copy-start.19
  1219.1 3.7 copy-start.18
  1219.1 5.7 copy-start.1
  (51 other events, 91.6 us)
Sparse Core Ops, SparseCore 0:
  24.7 83.0 all-gather.1
  594.6 77.0 reduce-scatter.1
  677.5 291.5 all-reduce.8
  974.8 237.4 all-reduce.6
